TPU v7x, 32 devices: a whole 2x2x4 slice. The times are simulated.
32 devices in a mesh: groups: 2 (over y), frames: 4 (over z), rows: 2 (over x), heads: 2 (over core).
Axes of the slice: x: 2, y: 2, z: 4, core: 2. Of those that a mesh axis runs over, the one named last changes fastest.
Arguments:
- clip_latent: bfloat16 [8, 12, 48, 640], P(('groups', 'frames'), 'rows', None, 'heads'), parts along dimension 0, may hold values from -40 to 40, as said below
- norm_gain: float32 [640], replicated, may hold values from 0.1 to 1.9
- w_time: bfloat16 [3, 640, 640], replicated, may hold values from -0.125 to 0.125
- w_query: bfloat16 [640, 640], P(None, 'heads'), may hold values from -0.7109375 to 0.7109375
- w_key: bfloat16 [640, 640], P(None, 'heads'), may hold values from -0.25 to 0.25
- w_value: bfloat16 [640, 640], P(None, 'heads'), may hold values from -0.25 to 0.25
- w_out: bfloat16 [640, 640], P('heads'), may hold values from -0.25 to 0.25
- reference_tokens: bfloat16 [288, 640], P(('groups', 'frames', 'rows'), 'heads'), parts along dimension 0, may hold values from -160 to 160, as said below
Outputs:
- block_out: bfloat16 [8, 12, 48, 640], P(('groups', 'frames'), 'rows', None, 'heads'), parts along dimension 0
There are 2 independent parts, one for each index of `groups`. A program takes and returns all parts, laid end to end along the dimension named above; an argument that names none is the same for every part. Nothing has to cross between parts.
Inputs may be any that keep to these rules, and one draw needn't show every extreme that they name: `clip_latent`: Real-valued latent features; each channel and each position has its own scale. `reference_tokens`: Real-valued reference features.
All inputs are finite; a program needn't handle non-finite values.
Results may differ from a plain program's by a relative error of at most 0.022.
Values may be sent and summed in bfloat16 or wider, within the bound.
A program may use at most 64 MiB of HBM per device.

v0:
```python
import jax
import jax.numpy as jnp
from jax import lax
from jax.sharding import PartitionSpec as P

C = 640
HEADS = 8


def with_halo(block, sides, width):
    for axis, dim in sides:
        count = lax.axis_size(axis)
        forward = [(i, i + 1) for i in range(count - 1)]
        backward = [(target, source) for source, target in forward]
        low = lax.ppermute(
            lax.slice_in_dim(block, block.shape[dim] - width, None, axis=dim), axis, forward
        )
        high = lax.ppermute(lax.slice_in_dim(block, 0, width, axis=dim), axis, backward)
        block = jnp.concatenate([low, block, high], axis=dim)
    return block


def temporal_terms(padded, weights, frames_here):
    summed = jnp.dot(padded[0:frames_here], weights[0], preferred_element_type=jnp.float32)
    summed = summed + jnp.dot(
        padded[1 : 1 + frames_here], weights[1], preferred_element_type=jnp.float32
    )
    summed = summed + jnp.dot(
        padded[2 : 2 + frames_here], weights[2], preferred_element_type=jnp.float32
    )
    return summed


def attend_head(operands):
    query_head, key_head, value_head = operands
    scores = jnp.dot(query_head, key_head.T, preferred_element_type=jnp.float32)
    top = jnp.max(scores, axis=1, keepdims=True)
    expo = jnp.exp(scores - top)
    total = jnp.sum(expo, axis=1, keepdims=True)
    probs = expo.astype(jnp.bfloat16)
    return (jnp.dot(probs, value_head, preferred_element_type=jnp.float32) / total).astype(
        jnp.bfloat16
    )


def body(clip_latent, norm_gain, w_time, w_query, w_key, w_value, w_out, reference_tokens):
    frames_here, rows_here, cols_here, half_width = clip_latent.shape
    head_size = C // HEADS
    local_heads = half_width // head_size
    position = lax.axis_index("heads")
    padded_half = with_halo(clip_latent, (("frames", 0),), 1)
    padded = lax.all_gather(padded_half, "heads", axis=3, tiled=True)
    summed = temporal_terms(padded, w_time, frames_here)
    temporal_full = (padded[1 : 1 + frames_here].astype(jnp.float32) + summed).astype(jnp.bfloat16)
    temporal_half = lax.dynamic_slice_in_dim(temporal_full, position * half_width, half_width, 3)
    feats = temporal_full.astype(jnp.float32)
    centre = jnp.mean(feats, axis=-1, keepdims=True)
    spread = jnp.mean((feats - centre) ** 2, axis=-1, keepdims=True)
    normed = ((feats - centre) * lax.rsqrt(spread + 1e-05) * norm_gain).astype(jnp.bfloat16)
    scale = 1.0 / jnp.sqrt(jnp.float32(head_size))
    query = (jnp.dot(normed, w_query, preferred_element_type=jnp.float32) * scale).astype(
        jnp.bfloat16
    )
    ref_full = lax.all_gather(reference_tokens, "heads", axis=1, tiled=True)
    w_both = jnp.concatenate([w_key, w_value], axis=1)
    key_value = lax.all_gather(
        jnp.dot(ref_full, w_both, preferred_element_type=jnp.float32).astype(jnp.bfloat16),
        ("frames", "rows"),
        axis=0,
        tiled=True,
    )
    key_heads = key_value[:, :half_width].reshape(-1, local_heads, head_size).transpose(1, 0, 2)
    value_heads = key_value[:, half_width:].reshape(-1, local_heads, head_size).transpose(1, 0, 2)
    query_heads = query.reshape(-1, local_heads, head_size).transpose(1, 0, 2)
    attended = lax.map(attend_head, (query_heads, key_heads, value_heads))
    attended = attended.transpose(1, 0, 2).reshape(frames_here, rows_here, cols_here, half_width)
    partial_out = jnp.dot(attended, w_out, preferred_element_type=jnp.float32)
    summed_out = lax.psum_scatter(partial_out, "heads", scatter_dimension=3, tiled=True)
    return (temporal_half.astype(jnp.float32) + summed_out).astype(jnp.bfloat16)


def solution(mesh):
    return jax.shard_map(
        body,
        mesh=mesh,
        in_specs=(
            P(("groups", "frames"), "rows", None, "heads"),
            P(),
            P(),
            P(None, "heads"),
            P(None, "heads"),
            P(None, "heads"),
            P("heads", None),
            P(("groups", "frames", "rows"), "heads"),
        ),
        out_specs=P(("groups", "frames"), "rows", None, "heads"),
        check_vma=False,
    )
```

profile of v0, /device:TPU:0, one launch (start us, length us, event | category | flops | bytes accessed | tf_op | source)
XLA Modules:
  0.0 101.4 jit_solution(3994693648743988713)
XLA Ops:
  6.5 5.1 %collective-permute-start = (bf16[1,6,48,320]{3,2,1,0:T(8,128)(2,1)}, bf16[1,6,48,320]{3,2,1,0:T(8,128)(2,1)S(1)}, u32[]{:S(2)}, u32[]{:S(2)}) collective-permute-start(bf16[1,6,48,320]{3,2,1,0:T(8,128)(2,1)} %param.10), channel_id=1, source_target_pairs={{0,4},{4,8},{8,12},{1,5},{5,9},{9,13},{2,6},{6,10},{10,14},{3,7},{... | collective-permute-start | bytes 552968 | tf_op jit(solution)/shard_map/ppermute | solution.py:15
  11.6 1.3 %collective-permute-start.1 = (bf16[1,6,48,320]{3,2,1,0:T(8,128)(2,1)}, bf16[1,6,48,320]{3,2,1,0:T(8,128)(2,1)S(1)}, u32[]{:S(2)}, u32[]{:S(2)}) collective-permute-start(bf16[1,6,48,320]{3,2,1,0:T(8,128)(2,1)} %param.10), channel_id=1, source_target_pairs={{4,0},{8,4},{12,8},{5,1},{9,5},{13,9},{6,2},{10,6},{14,10},{7,3},{... | collective-permute-start | bytes 552968 | tf_op jit(solution)/shard_map/ppermute | solution.py:18
  12.9 3.7 %collective-permute-done = bf16[1,6,48,320]{3,2,1,0:T(8,128)(2,1)S(1)} collective-permute-done((bf16[1,6,48,320]{3,2,1,0:T(8,128)(2,1)}, bf16[1,6,48,320]{3,2,1,0:T(8,128)(2,1)S(1)}, u32[]{:S(2)}, u32[]{:S(2)}) %collective-permute-start) | collective-permute-done | bytes 184352 | tf_op jit(solution)/shard_map/ppermute | solution.py:15
  16.6 4.0 %collective-permute-done.1 = bf16[1,6,48,320]{3,2,1,0:T(8,128)(2,1)S(1)} collective-permute-done((bf16[1,6,48,320]{3,2,1,0:T(8,128)(2,1)}, bf16[1,6,48,320]{3,2,1,0:T(8,128)(2,1)S(1)}, u32[]{:S(2)}, u32[]{:S(2)}) %collective-permute-start.1) | collective-permute-done | bytes 184352 | tf_op jit(solution)/shard_map/ppermute | solution.py:18
  20.6 1.1 %pad_maximum_fusion = bf16[3,6,48,320]{3,2,1,0:T(8,128)(2,1)S(1)} fusion(bf16[1,6,48,320]{3,2,1,0:T(8,128)(2,1)S(1)} %collective-permute-done.1, bf16[1,6,48,320]{3,2,1,0:T(8,128)(2,1)} %param.10, bf16[1,6,48,320]{3,2,1,0:T(8,128)(2,1)S(1)} %collective-permute-done), kind=kLoop, calls=%fused_computation.44 | loop fusion | flops 552960 | bytes 1105920 | tf_op jit(solution)/shard_map/concatenate | solution.py:19
  21.8 2.6 %copy.27 = bf16[3,6,48,320]{2,1,0,3:T(8,128)(2,1)} copy(bf16[3,6,48,320]{3,2,1,0:T(8,128)(2,1)S(1)} %pad_maximum_fusion) | data formatting | bytes 1105920 | tf_op jit(solution)/shard_map/concatenate | solution.py:19
  24.5 1.8 %all-gather = bf16[2,320,18]{1,2,0:T(8,128)(2,1)S(1)} all-gather(bf16[1,320,18]{1,2,0:T(8,128)(2,1)S(1)} %bitcast.90), channel_id=1, replica_groups=mesh['groups'=2,'frames'=4,'rows'=2,'heads'=2] {'heads'}, dimensions={0}, use_global_device_ids=true | all-gather | bytes 34560 | tf_op jit(solution)/shard_map/all_gather | solution.py:64
  26.9 30.8 %all-gather.1 = bf16[8,18,640]{2,1,0:T(8,128)(2,1)S(1)} all-gather(bf16[1,18,640]{2,1,0:T(8,128)(2,1)S(1)} %fusion.20), channel_id=1, replica_groups=mesh['groups'=2,'frames'=4,'rows'=2,'heads'=2] {'frames','rows'}, dimensions={0}, use_global_device_ids=true | all-gather | bytes 207360 | tf_op jit(solution)/shard_map/all_gather | solution.py:66
  58.8 3.8 %fusion.48 = (bf16[1,6,48,640]{2,1,0,3:T(8,128)(2,1)S(1)}, bf16[1,6,48,640]{2,1,0,3:T(8,128)(2,1)S(1)}, bf16[1,6,48,640]{2,1,0,3:T(8,128)(2,1)}) fusion(bf16[3,6,48,640]{2,1,0,3:T(8,128)(2,1)} %all-gather.4.cloned.1.call-done), kind=kLoop, calls=%fused_computation.59 | loop fusion | bytes 2211840 | tf_op jit(solution)/shard_map/slice | solution.py:29
  62.7 1.9 %copy.38 = bf16[1,6,48,640]{3,2,1,0:T(8,128)(2,1)S(1)} copy(bf16[1,6,48,640]{2,1,0,3:T(8,128)(2,1)} %get-tuple-element.62) | data formatting | bytes 737280
  64.6 1.7 %copy.39 = bf16[1,6,48,640]{3,2,1,0:T(8,128)(2,1)} copy(bf16[1,6,48,640]{2,1,0,3:T(8,128)(2,1)S(1)} %get-tuple-element.61) | data formatting | bytes 737280
  66.3 1.1 %copy.40 = bf16[1,6,48,640]{3,2,1,0:T(8,128)(2,1)S(1)} copy(bf16[1,6,48,640]{2,1,0,3:T(8,128)(2,1)S(1)} %get-tuple-element.60) | data formatting | bytes 737280
  67.4 1.8 %fusion.28 = f32[6,48,640]{2,1,0:T(8,128)S(1)} fusion(bf16[3,640,640]{2,1,0:T(8,128)(2,1)} %param.12, bf16[1,6,48,640]{3,2,1,0:T(8,128)(2,1)} %copy.39), kind=kOutput, calls=%fused_computation.36 | convolution fusion | flops 235929600 | bytes 1925120 | tf_op jit(solution)/shard_map/dot_general | solution.py:24
  69.2 1.6 %convolution_add_fusion.1 = f32[6,48,640]{2,1,0:T(8,128)S(1)} fusion(f32[6,48,640]{2,1,0:T(8,128)S(1)} %fusion.28, bf16[3,640,640]{2,1,0:T(8,128)(2,1)} %param.12, bf16[1,6,48,640]{3,2,1,0:T(8,128)(2,1)S(1)} %copy.38), kind=kOutput, calls=%fused_computation.20 | convolution fusion | flops 236113920 | bytes 2662400 | tf_op jit(solution)/shard_map/dot_general | solution.py:25
  70.9 1.8 %convert_reduce_fusion = (f32[6,48]{1,0:T(8,128)S(1)}, bf16[1,6,48,640]{3,2,1,0:T(8,128)(2,1)S(1)}) fusion(f32[6,48,640]{2,1,0:T(8,128)S(1)} %convolution_add_fusion.1, bf16[3,640,640]{2,1,0:T(8,128)(2,1)} %param.12, bf16[1,6,48,640]{3,2,1,0:T(8,128)(2,1)S(1)} %copy.40, bf16[1,6,48,640]{3,2,1,0:T(8,128)(2,1)S(1)} %copy.38), kind=kOutput, calls=%fused_computation.28 | convolution fusion | flops 237035232 | bytes 2663552 | tf_op jit(solution)/shard_map/dot_general | solution.py:28
  73.6 5.1 %while.10 = (s32[]{:T(128)}, bf16[4,288,80]{1,2,0:T(8,128)(2,1)S(1)}, bf16[4,288,80]{2,1,0:T(8,128)(2,1)S(1)}, bf16[4,144,80]{2,1,0:T(8,128)(2,1)S(1)}, bf16[4,144,80]{2,1,0:T(8,128)(2,1)}, /*index=5*/s32[]{:T(128)}) while((s32[]{:T(128)}, bf16[4,288,80]{1,2,0:T(8,128)(2,1)S(1)}, bf16[4,288,80]{2,1,0:T(8,128)(2,1)S(1)}, ...), condition=%wide.region_5.6_spmd, body=%wide.region_2.5_spmd.sunk | while | flops 13523906 | bytes 771525 | solution.py:75
  75.2 1.0 fusion.61
  76.5 1.0 fusion.61
  77.8 1.0 fusion.61
  79.2 1.2 %convolution_bitcast_fusion = f32[1,6,48,640]{3,2,1,0:T(8,128)} fusion(bf16[6,48,320]{2,1,0:T(8,128)(2,1)S(1)} %reshape.70, bf16[320,640]{1,0:T(8,128)(2,1)S(1)} %copy-done), kind=kOutput, calls=%fused_computation.17 | convolution fusion | flops 117964800 | bytes 1331200 | tf_op jit(solution)/shard_map/dot_general | solution.py:77
  80.5 2.2 %copy.36 = f32[1,6,48,640]{2,1,0,3:T(8,128)S(1)} copy(f32[1,6,48,640]{3,2,1,0:T(8,128)} %convolution_bitcast_fusion) | data formatting | bytes 1474560
  82.7 1.5 %reshape.80 = f32[640,288]{1,0:T(8,128)} reshape(f32[640,1,6,48]{3,2,1,0:T(8,128)S(1)} %bitcast.84) | data formatting | bytes 1474560
  84.2 7.7 %reduce-scatter.4.cloned.1.call-done = f32[320,288]{1,0:T(8,128)} async-done(((f32[640,288]{1,0:T(8,128)}), f32[320,288]{1,0:T(8,128)}) %reduce-scatter.4.cloned.1.call-update) | async-done | bytes 368656
  91.9 1.4 %reshape.81 = f32[320,1,6,48]{3,2,1,0:T(8,128)S(1)} reshape(f32[320,288]{1,0:T(8,128)} %reduce-scatter.4.cloned.1.call-done) | data formatting | bytes 737280
  (48 shorter events, 6.4 us)
Async XLA Ops:
  6.5 72.7 %copy-start = (bf16[320,640]{1,0:T(8,128)(2,1)S(1)}, bf16[320,640]{1,0:T(8,128)(2,1)}, u32[]{:S(2)}) copy-start(bf16[320,640]{1,0:T(8,128)(2,1)} %param.16) | copy-start | bytes 1228804
  6.5 52.3 %all-gather.4.cloned.1.call-start = ((), (), s32[]{:S(2)}) async-start(), calls=%async_computation.1 | async-start | bytes 5898240 | tf_op jit(solution)/shard_map/all_gather | solution.py:52
  6.5 10.1 %collective-permute-start = (bf16[1,6,48,320]{3,2,1,0:T(8,128)(2,1)}, bf16[1,6,48,320]{3,2,1,0:T(8,128)(2,1)S(1)}, u32[]{:S(2)}, u32[]{:S(2)}) collective-permute-start(bf16[1,6,48,320]{3,2,1,0:T(8,128)(2,1)} %param.10), channel_id=1, source_target_pairs={{0,4},{4,8},{8,12},{1,5},{5,9},{9,13},{2,6},{6,10},{10,14},{3,7},{... | collective-permute-start | bytes 552968 | tf_op jit(solution)/shard_map/ppermute | solution.py:15
  11.6 9.0 %collective-permute-start.1 = (bf16[1,6,48,320]{3,2,1,0:T(8,128)(2,1)}, bf16[1,6,48,320]{3,2,1,0:T(8,128)(2,1)S(1)}, u32[]{:S(2)}, u32[]{:S(2)}) collective-permute-start(bf16[1,6,48,320]{3,2,1,0:T(8,128)(2,1)} %param.10), channel_id=1, source_target_pairs={{4,0},{8,4},{12,8},{5,1},{9,5},{13,9},{6,2},{10,6},{14,10},{7,3},{... | collective-permute-start | bytes 552968 | tf_op jit(solution)/shard_map/ppermute | solution.py:18
  21.7 2.8 %copy-start.2 = (bf16[18,320]{1,0:T(8,128)(2,1)S(1)}, bf16[18,320]{1,0:T(8,128)(2,1)}, u32[]{:S(2)}) copy-start(bf16[18,320]{1,0:T(8,128)(2,1)} %param.17) | copy-start | bytes 34564
  21.7 4.7 %copy-start.3 = (bf16[640,320]{0,1:T(8,128)(2,1)S(1)}, bf16[640,320]{0,1:T(8,128)(2,1)}, u32[]{:S(2)}) copy-start(bf16[640,320]{0,1:T(8,128)(2,1)} %param.15) | copy-start | bytes 1228804
  21.7 4.7 %copy-start.4 = (bf16[640,320]{0,1:T(8,128)(2,1)S(1)}, bf16[640,320]{0,1:T(8,128)(2,1)}, u32[]{:S(2)}) copy-start(bf16[640,320]{0,1:T(8,128)(2,1)} %param.14) | copy-start | bytes 1228804
  24.4 67.5 %reduce-scatter.4.cloned.1.call-start = ((), (), s32[]{:S(2)}) async-start(), calls=%async_computation.2 | async-start | bytes 1474560
  70.8 2.1 %copy-start.5 = (bf16[640,320]{0,1:T(8,128)(2,1)S(1)}, bf16[640,320]{0,1:T(8,128)(2,1)}, u32[]{:S(2)}) copy-start(bf16[640,320]{0,1:T(8,128)(2,1)} %param.13) | copy-start | bytes 1228804
  70.8 2.1 %copy-start.6 = (f32[640]{0:T(1024)S(1)}, f32[640]{0:T(1024)}, u32[]{:S(2)}) copy-start(f32[640]{0:T(1024)} %param.11) | copy-start | bytes 7684
  72.6 1.0 copy-start.1
Sparse Core Ops, SparseCore 0:
  24.5 13.4 all-gather.3
  84.3 7.5 reduce-scatter.3
where the time goes:
time: 102 us; the launch traced here: 101 us
  blocking collectives  32.6 us (32%)
  local copies, waits for them, and re-layouts  18.7 us (18%)
  waiting for transfers between devices  15.4 us (15%)
  between operations  13.7 us (13%)
  matrix products  12 us (12%)
  starting transfers between devices  6.42 us (6%)
  other arithmetic  2.41 us (2%)
    all_gather x1, blocking collectives, body(): lax.all_gather(jnp.dot(ref_full, w_both, preferred_element_type=jnp.float...  30.8 us
    unnamed x23, local copies, waits for them, and re-layouts  10.5 us
    unnamed x3, waiting for transfers between devices  7.71 us
    ppermute x1, starting transfers between devices, with_halo(): lax.ppermute(lax.slice_in_dim(block, block.shape[dim] - width, None, axis...  5.09 us
    ppermute x1, waiting for transfers between devices, with_halo(): lax.ppermute(lax.slice_in_dim(block, 0, width, axis=dim), axis, backward)  4.02 us
    dot_general x4, matrix products, attend_head(): jnp.dot(probs, value_head, preferred_element_type=jnp.float32) / total  3.96 us
    slice x1, local copies, waits for them, and re-layouts, temporal_terms(): padded[2:2 + frames_here]  3.84 us
    ppermute x1, waiting for transfers between devices, with_halo(): lax.ppermute(lax.slice_in_dim(block, block.shape[dim] - width, None, axis...  3.67 us
  transfers between devices with their start and end apart: 4, of which 3 were waited for; matrix products, arithmetic and copies ran while one was open for 2% of the time, Pallas kernels for 0%

commit v1 on v0

v1 whole, which is shorter than its diff:
```python
import functools

import jax
import jax.numpy as jnp
from jax import lax
from jax.experimental import pallas as pl
from jax.experimental.pallas import tpu as pltpu
from jax.sharding import PartitionSpec as P

HEAD_SIZE = 80
BF16 = jnp.bfloat16
F32 = jnp.float32
MESH = pl.DeviceIdType.MESH


def dot(a, b):
    return jnp.dot(a, b, preferred_element_type=F32)


def kernel(
    sizes,
    clip, gain, w_time, w_query, w_key, w_value, w_out, tokens,
    out,
    x, wt, wq, wk, wv, wo, wo_half, gains, slots, tok, keys, values, base, att,
    local_sem, halo_send, halo_recv, relay_send, relay_recv, pair_send, pair_recv,
    near_send, near_recv, far_send, far_recv, att_send, att_recv,
):
    nf, nr, nh, chunks, pad = sizes
    positions, half = clip.shape
    count = tokens.shape[0]
    local_heads = half // HEAD_SIZE
    step = positions // chunks
    f, r, h = lax.axis_index("frames"), lax.axis_index("rows"), lax.axis_index("heads")
    other = 1 - h
    partner = {"heads": other}

    def remote(src, dst, send, recv, to):
        return pltpu.make_async_remote_copy(
            src_ref=src, dst_ref=dst, send_sem=send, recv_sem=recv, device_id=to, device_id_type=MESH
        )

    def rows_of(c):
        return pl.ds(c * step, step)

    barrier = pltpu.get_barrier_semaphore()
    plane = [(a, b) for a in range(nr) for b in range(nh) if (a, b) != (0, 0)]

    def plane_to(a, b):
        return {"rows": lax.rem(r + a, nr), "heads": lax.rem(h + b, nh)}

    for a, b in plane:
        pl.semaphore_signal(barrier, inc=1, device_id=plane_to(a, b), device_id_type=MESH)
    for d in range(1, nf):
        pl.semaphore_signal(barrier, inc=1, device_id={"frames": lax.rem(f + d, nf)}, device_id_type=MESH)

    mine = r * nf + f
    loads = [
        pltpu.make_async_copy(src, dst, local_sem.at[i])
        for i, (src, dst) in enumerate(
            [
                (tokens, slots.at[h, mine]),
                (clip, x.at[1, h]),
                (w_time, wt),
                (w_out, wo.at[0]),
                (w_key, wk),
                (w_value, wv),
                (w_query, wq),
                (gain, gains),
            ]
        )
    ]
    for load in loads:
        load.start()

    tok[...] = jnp.zeros_like(tok)

    @pl.when(f == 0)
    def _():
        x[0] = jnp.zeros(x.shape[1:], BF16)

    @pl.when(f == nf - 1)
    def _():
        x[2] = jnp.zeros(x.shape[1:], BF16)

    pl.semaphore_wait(barrier, len(plane) + nf - 1)

    near = [
        remote(tokens, slots.at[h, mine], near_send.at[d], near_recv.at[d], {"frames": lax.rem(f + d, nf)})
        for d in range(1, nf)
    ]
    for copy in near:
        copy.start()

    def halo(side, c):
        to = f + 1 if side == 0 else f - 1
        slot = 0 if side == 0 else 2
        return remote(
            clip.at[rows_of(c)], x.at[slot, h, rows_of(c)], halo_send.at[side, c], halo_recv.at[side, c],
            {"frames": to},
        )

    def relay(side, c):
        slot = 0 if side == 0 else 2
        ref = x.at[slot, h, rows_of(c)]
        return remote(ref, ref, relay_send.at[side, c], relay_recv.at[side, c], partner)

    sends = (f < nf - 1, f > 0)
    gets = (f > 0, f < nf - 1)
    for c in range(chunks):
        for side in range(2):
            @pl.when(sends[side])
            def _():
                halo(side, c).start()

    pair = [
        remote(clip, x.at[1, h], pair_send.at[0], pair_recv.at[0], partner),
        remote(w_out, wo.at[1], pair_send.at[1], pair_recv.at[1], partner),
    ]
    for copy in pair:
        copy.start()

    def weight(o, which):
        return wt[o, pl.ds(pl.multiple_of(which * half, half), half), :]

    loads[1].wait()
    loads[2].wait()
    pair[0].wait_recv()
    first = jnp.concatenate([x[1, 0].astype(F32), x[1, 1].astype(F32)], axis=1)
    base[...] = first + dot(x[1, 0], wt[1, :half, :]) + dot(x[1, 1], wt[1, half:, :])

    loads[3].wait()
    pair[1].wait_recv()
    for k in range(2):
        whole = wo[k].astype(F32)
        wo_half[k] = jnp.where(h == 0, whole[:, :half], whole[:, half:]).astype(BF16)

    loads[0].wait()
    for copy in near:
        copy.wait_recv()
    line = slots.at[h, pl.ds(r * nf, nf)]
    far = [remote(line, line, far_send.at[a, b], far_recv.at[a, b], plane_to(a, b)) for a, b in plane]
    for copy in far:
        copy.start()

    def arrive(c):
        for side in range(2):
            @pl.when(gets[side])
            def _():
                halo(side, c).wait_recv()
                relay(side, c).start()
        rows = rows_of(c)
        base[rows] = base[rows] + dot(x[0, h, rows], weight(0, h)) + dot(x[2, h, rows], weight(2, h))

    def make_keys():
        for copy in far:
            copy.wait_recv()
        for k in range(nh):
            if nr * nf <= 16:
                for i in range(nr * nf):
                    tok[k, pl.ds(i * pad, count), :] = slots[k, i]
            else:
                def place(i, carry):
                    tok[k, pl.ds(pl.multiple_of(i * pad, pad), count), :] = slots[k, i]
                    return carry

                lax.fori_loop(0, nr * nf, place, 0)
        loads[4].wait()
        loads[5].wait()
        block = min(256, tok.shape[1])

        def project(i, carry):
            at = pl.ds(pl.multiple_of(i * block, block), block)
            head = lax.broadcasted_iota(jnp.int32, (block, half), 1)
            for weights, dest in ((wk, keys), (wv, values)):
                full = dot(tok[0, at, :], weights[:half, :]) + dot(tok[1, at, :], weights[half:, :])
                for k in range(local_heads):
                    inside = (head >= k * HEAD_SIZE) & (head < (k + 1) * HEAD_SIZE)
                    dest[k, at, :] = jnp.where(inside, full, 0.0).astype(BF16)
            return carry

        trips = tok.shape[1] // block
        if trips == 1:
            project(0, 0)
        else:
            lax.fori_loop(0, trips, project, 0)
        loads[6].wait()
        loads[7].wait()

    scale = 1.0 / (HEAD_SIZE ** 0.5)

    def attended(c):
        return remote(att.at[0, rows_of(c)], att.at[1, rows_of(c)], att_send.at[c], att_recv.at[c], partner)

    def process(c):
        rows = rows_of(c)
        for side in range(2):
            @pl.when(gets[side])
            def _():
                relay(side, c).wait_recv()
        summed = base[rows] + dot(x[0, other, rows], weight(0, other)) + dot(x[2, other, rows], weight(2, other))
        feats = summed.astype(BF16).astype(F32)
        base[rows] = feats
        centre = jnp.mean(feats, axis=-1, keepdims=True)
        moved = feats - centre
        spread = jnp.mean(moved * moved, axis=-1, keepdims=True)
        normed = (moved * lax.rsqrt(spread + 1e-05) * gains[...]).astype(BF16)
        query = (dot(normed, wq[...]) * scale).astype(BF16)
        total_tokens = tok.shape[1]
        column = lax.broadcasted_iota(jnp.int32, (step, total_tokens), 1)
        valid = lax.rem(column, pad) < count
        result = jnp.zeros((step, half), F32)
        for k in range(local_heads):
            scores = lax.dot_general(query, keys[k], (((1,), (1,)), ((), ())), preferred_element_type=F32)
            scores = jnp.where(valid, scores, -3e38)
            expo = jnp.exp(scores - jnp.max(scores, axis=1, keepdims=True))
            total = jnp.sum(expo, axis=1, keepdims=True)
            result = result + dot(expo.astype(BF16), values[k]) * (1.0 / total)
        att[0, rows] = result.astype(BF16)
        attended(c).start()

    def finish(c):
        rows = rows_of(c)
        feats = base[rows]
        own = jnp.where(h == 0, feats[:, :half], feats[:, half:])
        mixed = own + dot(att[0, rows], wo_half[0])
        attended(c).wait_recv()
        out[rows] = (mixed + dot(att[1, rows], wo_half[1])).astype(BF16)

    arrive(0)
    for c in range(1, min(2, chunks)):
        arrive(c)
    make_keys()
    for c in range(chunks):
        process(c)
        if c + 2 < chunks:
            arrive(c + 2)
        if c >= 1:
            finish(c - 1)
    finish(chunks - 1)

    for copy in near + pair + far:
        copy.wait_send()
    for c in range(chunks):
        attended(c).wait_send()
        for side in range(2):
            @pl.when(sends[side])
            def _():
                halo(side, c).wait_send()

            @pl.when(gets[side])
            def _():
                relay(side, c).wait_send()


def body(sizes, clip_latent, norm_gain, w_time, w_query, w_key, w_value, w_out, reference_tokens):
    nf, nr, nh = sizes
    shape = clip_latent.shape
    half, width = w_out.shape
    positions = shape[0] * shape[1] * shape[2]
    assert shape[0] == 1 and nh == 2
    chunks = next(n for n in (3, 2, 1) if positions % (16 * n) == 0)
    count = reference_tokens.shape[0]
    pad = -(-count // 16) * 16
    total = pad * nf * nr
    heads = half // HEAD_SIZE
    dma = pltpu.SemaphoreType.DMA
    result = pl.pallas_call(
        functools.partial(kernel, (nf, nr, nh, chunks, pad)),
        out_shape=jax.ShapeDtypeStruct((positions, half), BF16),
        in_specs=[pl.BlockSpec(memory_space=pl.ANY)] * 8,
        out_specs=pl.BlockSpec(memory_space=pltpu.VMEM),
        scratch_shapes=[
            pltpu.VMEM((3, 2, positions, half), BF16),
            pltpu.VMEM(w_time.shape, BF16),
            pltpu.VMEM(w_query.shape, BF16),
            pltpu.VMEM(w_key.shape, BF16),
            pltpu.VMEM(w_value.shape, BF16),
            pltpu.VMEM((2, half, width), BF16),
            pltpu.VMEM((2, half, half), BF16),
            pltpu.VMEM((1, width), F32),
            pltpu.VMEM((nh, nr * nf, count, half), BF16),
            pltpu.VMEM((nh, total, half), BF16),
            pltpu.VMEM((heads, total, half), BF16),
            pltpu.VMEM((heads, total, half), BF16),
            pltpu.VMEM((positions, width), F32),
            pltpu.VMEM((2, positions, half), BF16),
            dma((8,)),
            dma((2, chunks)),
            dma((2, chunks)),
            dma((2, chunks)),
            dma((2, chunks)),
            dma((2,)),
            dma((2,)),
            dma((nf,)),
            dma((nf,)),
            dma((nr, nh)),
            dma((nr, nh)),
            dma((chunks,)),
            dma((chunks,)),
        ],
        compiler_params=pltpu.CompilerParams(collective_id=0, has_side_effects=True),
    )(
        clip_latent.reshape(positions, half),
        norm_gain.reshape(1, width),
        w_time, w_query, w_key, w_value, w_out, reference_tokens,
    )
    return result.reshape(shape)


def solution(mesh):
    sizes = (mesh.shape["frames"], mesh.shape["rows"], mesh.shape["heads"])
    return jax.shard_map(
        functools.partial(body, sizes),
        mesh=mesh,
        in_specs=(
            P(("groups", "frames"), "rows", None, "heads"),
            P(),
            P(),
            P(None, "heads"),
            P(None, "heads"),
            P(None, "heads"),
            P("heads", None),
            P(("groups", "frames", "rows"), "heads"),
        ),
        out_specs=P(("groups", "frames"), "rows", None, "heads"),
        check_vma=False,
    )
```

time: 102 us -> 32.1 us (0.31)
  blocking collectives: 32.6 us -> 0 us
  Pallas kernels: 0 us -> 22.9 us
  waiting for transfers between devices: 15.4 us -> 0 us
  between operations: 13.7 us -> 0.01 us
  matrix products: 12 us -> 0 us
  local copies, waits for them, and re-layouts: 18.7 us -> 8.88 us
  starting transfers between devices: 6.42 us -> 0 us
  other arithmetic: 2.41 us -> 0 us
    all_gather x2 -> x0, blocking collectives: 32.6 us -> none  [the longest x1 30.8 us: body(): lax.all_gather(jnp.dot(ref_full, w_both, preferred_element_type=jnp.float...]
    pallas_call x0 -> x1, Pallas kernels: none -> 22.9 us  [body(): pl.pallas_call(functools.partial(kernel, (nf, nr, nh, chunks, pad)), out_...]
    dot_general x14 -> x0, matrix products: 12 us -> none  [the longest x4 3.96 us: attend_head(): jnp.dot(probs, value_head, preferred_element_type=jnp.float32) / total]
    unnamed x3 -> x0, waiting for transfers between devices: 7.71 us -> none
    ppermute x2 -> x0, waiting for transfers between devices: 7.69 us -> none  [the longest x1 4.02 us: with_halo(): lax.ppermute(lax.slice_in_dim(block, 0, width, axis=dim), axis, backward)]
    ppermute x2 -> x0, starting transfers between devices: 6.38 us -> none  [the longest x1 5.09 us: with_halo(): lax.ppermute(lax.slice_in_dim(block, block.shape[dim] - width, None, axis...]
    slice x2 -> x0, local copies, waits for them, and re-layouts: 3.94 us -> none  [the longest x1 3.84 us: temporal_terms(): padded[2:2 + frames_here]]
    unnamed x23 -> x4, local copies, waits for them, and re-layouts: 10.5 us -> 7.61 us
  transfers between devices with their start and end apart: 4 -> 0, of which waited for: 3 -> 0; matrix products, arithmetic and copies ran while one was open for 2% -> 0% of each run, Pallas kernels for 0% -> 0%
where the time goes in v1:
time: 32.1 us; the launch traced here: 31.8 us
  Pallas kernels  22.9 us (71%)
  local copies, waits for them, and re-layouts  8.88 us (28%)
    pallas_call x1, Pallas kernels, body(): pl.pallas_call(functools.partial(kernel, (nf, nr, nh, chunks, pad)), out_...  22.9 us
    unnamed x4, local copies, waits for them, and re-layouts  7.61 us
    reshape x1, local copies, waits for them, and re-layouts, body(): norm_gain.reshape(1, width)  1.27 us

profile of v1, /device:TPU:0, one launch (start us, length us, event | category | flops | bytes accessed | tf_op | source)
XLA Modules:
  0.0 31.8 jit_solution(1079233395528431049)
XLA Ops:
  0.0 1.3 %reshape.10.gain = f32[1,640]{1,0:T(1,128)} reshape(f32[640]{0:T(1024)} %param.9) | data formatting | bytes 5120 | tf_op jit(solution)/shard_map/reshape | solution.py:304
  1.3 2.0 %copy.9.w_query = bf16[640,320]{1,0:T(8,128)(2,1)} copy(bf16[640,320]{0,1:T(8,128)(2,1)} %param.11) | data formatting | bytes 819200 | tf_op args[3]
  3.2 2.0 %copy.10.w_key = bf16[640,320]{1,0:T(8,128)(2,1)} copy(bf16[640,320]{0,1:T(8,128)(2,1)} %param.12) | data formatting | bytes 819200 | tf_op args[4]
  5.2 2.0 %copy.11.w_value = bf16[640,320]{1,0:T(8,128)(2,1)} copy(bf16[640,320]{0,1:T(8,128)(2,1)} %param.13) | data formatting | bytes 819200 | tf_op args[5]
  7.2 22.9 %shard_map.82 = bf16[288,320]{1,0:T(8,128)(2,1)} custom-call(bf16[288,320]{1,0:T(8,128)(2,1)} %bitcast.3, f32[1,640]{1,0:T(1,128)} %reshape.10.gain, bf16[3,640,640]{2,1,0:T(8,128)(2,1)} %w_time.1, bf16[640,320]{1,0:T(8,128)(2,1)} %copy.9.w_query, bf16[640,320]{1,0:T(8,128)(2,1)} %copy.10.w_key, bf16[640,320]{1,0:T(8,128)(2,1)} %copy.11.w_value, ...), custom_call_target="tpu_custom_call" | custom-call | tf_op jit(solution)/shard_map/pallas_call | solution.py:267
  30.1 1.6 %copy.13 = bf16[1,6,48,320]{3,2,1,0:T(8,128)(2,1)} copy(bf16[1,6,48,320]{3,2,1,0:T(8,128)(2,1)} %bitcast.2) | data formatting | bytes 368640

commit v2 on v1

--- a/solution.py
+++ b/solution.py
@@ -11,6 +11,10 @@
 BF16 = jnp.bfloat16
 F32 = jnp.float32
 MESH = pl.DeviceIdType.MESH
+
+
+def dot_t(a, b):
+    return lax.dot_general(a, b, (((1,), (1,)), ((), ())), preferred_element_type=F32)
 
 
 def dot(a, b):
@@ -171,8 +175,9 @@
         def project(i, carry):
             at = pl.ds(pl.multiple_of(i * block, block), block)
             head = lax.broadcasted_iota(jnp.int32, (block, half), 1)
+            both = jnp.concatenate([tok[k, at, :] for k in range(nh)], axis=1)
             for weights, dest in ((wk, keys), (wv, values)):
-                full = dot(tok[0, at, :], weights[:half, :]) + dot(tok[1, at, :], weights[half:, :])
+                full = dot_t(both, weights[...])
                 for k in range(local_heads):
                     inside = (head >= k * HEAD_SIZE) & (head < (k + 1) * HEAD_SIZE)
                     dest[k, at, :] = jnp.where(inside, full, 0.0).astype(BF16)
@@ -184,7 +189,6 @@
         else:
             lax.fori_loop(0, trips, project, 0)
         loads[6].wait()
-        loads[7].wait()
 
     scale = 1.0 / (HEAD_SIZE ** 0.5)
 
@@ -203,18 +207,24 @@
         centre = jnp.mean(feats, axis=-1, keepdims=True)
         moved = feats - centre
         spread = jnp.mean(moved * moved, axis=-1, keepdims=True)
-        normed = (moved * lax.rsqrt(spread + 1e-05) * gains[...]).astype(BF16)
-        query = (dot(normed, wq[...]) * scale).astype(BF16)
+        normed = (moved * lax.rsqrt(spread + 1e-05) * gain_row).astype(BF16)
+        query = (dot_t(normed, wq[...]) * scale).astype(BF16)
         total_tokens = tok.shape[1]
         column = lax.broadcasted_iota(jnp.int32, (step, total_tokens), 1)
         valid = lax.rem(column, pad) < count
-        result = jnp.zeros((step, half), F32)
-        for k in range(local_heads):
-            scores = lax.dot_general(query, keys[k], (((1,), (1,)), ((), ())), preferred_element_type=F32)
-            scores = jnp.where(valid, scores, -3e38)
+
+        def attend(k, result):
+            scores = jnp.where(valid, dot_t(query, keys[k]), -3e38)
             expo = jnp.exp(scores - jnp.max(scores, axis=1, keepdims=True))
             total = jnp.sum(expo, axis=1, keepdims=True)
-            result = result + dot(expo.astype(BF16), values[k]) * (1.0 / total)
+            return result + dot(expo.astype(BF16), values[k]) * (1.0 / total)
+
+        result = jnp.zeros((step, half), F32)
+        if total_tokens <= 1024:
+            for k in range(local_heads):
+                result = attend(k, result)
+        else:
+            result = lax.fori_loop(0, local_heads, attend, result)
         att[0, rows] = result.astype(BF16)
         attended(c).start()
 
@@ -225,6 +235,9 @@
         mixed = own + dot(att[0, rows], wo_half[0])
         attended(c).wait_recv()
         out[rows] = (mixed + dot(att[1, rows], wo_half[1])).astype(BF16)
+
+    loads[7].wait()
+    gain_row = gains[...].reshape(1, -1)
 
     arrive(0)
     for c in range(1, min(2, chunks)):
@@ -272,12 +285,12 @@
         scratch_shapes=[
             pltpu.VMEM((3, 2, positions, half), BF16),
             pltpu.VMEM(w_time.shape, BF16),
-            pltpu.VMEM(w_query.shape, BF16),
-            pltpu.VMEM(w_key.shape, BF16),
-            pltpu.VMEM(w_value.shape, BF16),
+            pltpu.VMEM((half, width), BF16),
+            pltpu.VMEM((half, width), BF16),
+            pltpu.VMEM((half, width), BF16),
             pltpu.VMEM((2, half, width), BF16),
             pltpu.VMEM((2, half, half), BF16),
-            pltpu.VMEM((1, width), F32),
+            pltpu.VMEM((width,), F32),
             pltpu.VMEM((nh, nr * nf, count, half), BF16),
             pltpu.VMEM((nh, total, half), BF16),
             pltpu.VMEM((heads, total, half), BF16),
@@ -301,8 +314,8 @@
         compiler_params=pltpu.CompilerParams(collective_id=0, has_side_effects=True),
     )(
         clip_latent.reshape(positions, half),
-        norm_gain.reshape(1, width),
-        w_time, w_query, w_key, w_value, w_out, reference_tokens,
+        norm_gain,
+        w_time, w_query.T, w_key.T, w_value.T, w_out, reference_tokens,
     )
     return result.reshape(shape)
 

time: 32.1 us -> 24.7 us (0.77)
  local copies, waits for them, and re-layouts: 8.88 us -> 1.64 us
    unnamed x4 -> x1, local copies, waits for them, and re-layouts: 7.61 us -> 1.64 us
    reshape x1 -> x0, local copies, waits for them, and re-layouts: 1.27 us -> none  [body(): norm_gain.reshape(1, width)]
where the time goes in v2:
time: 24.7 us; the launch traced here: 24.6 us
  Pallas kernels  22.9 us (93%)
  local copies, waits for them, and re-layouts  1.64 us (7%)
    pallas_call x1, Pallas kernels, body(): pl.pallas_call(functools.partial(kernel, (nf, nr, nh, chunks, pad)), out_...  22.9 us
    unnamed x1, local copies, waits for them, and re-layouts  1.64 us

profile of v2, /device:TPU:0, one launch (start us, length us, event | category | flops | bytes accessed | tf_op | source)
XLA Modules:
  0.0 24.6 jit_solution(16867658486070455152)
XLA Ops:
  0.0 22.9 %shard_map.82 = bf16[288,320]{1,0:T(8,128)(2,1)} custom-call(bf16[288,320]{1,0:T(8,128)(2,1)} %bitcast.9, f32[640]{0:T(1024)} %gain.1, bf16[3,640,640]{2,1,0:T(8,128)(2,1)} %w_time.1, bf16[320,640]{1,0:T(8,128)(2,1)} %bitcast.6, bf16[320,640]{1,0:T(8,128)(2,1)} %bitcast.7, bf16[320,640]{1,0:T(8,128)(2,1)} %bitcast.8, bf16[320,640]{1,0:T(8,128)(2,1)} %w_out.1, ...), custom_call_target="tpu_custom_call" | custom-call | tf_op jit(solution)/shard_map/pallas_call | solution.py:280
  22.9 1.6 %copy.10 = bf16[1,6,48,320]{3,2,1,0:T(8,128)(2,1)} copy(bf16[1,6,48,320]{3,2,1,0:T(8,128)(2,1)} %bitcast.5) | data formatting | bytes 368640

commit v3 on v2

--- a/solution.py
+++ b/solution.py
@@ -8,6 +8,7 @@
 from jax.sharding import PartitionSpec as P
 
 HEAD_SIZE = 80
+LANES = 128
 BF16 = jnp.bfloat16
 F32 = jnp.float32
 MESH = pl.DeviceIdType.MESH
@@ -25,7 +26,7 @@
     sizes,
     clip, gain, w_time, w_query, w_key, w_value, w_out, tokens,
     out,
-    x, wt, wq, wk, wv, wo, wo_half, gains, slots, tok, keys, values, base, att,
+    x, wt, wq, wkv, wo, wo_half, gains, slots, tok, keys, values, base, att,
     local_sem, halo_send, halo_recv, relay_send, relay_recv, pair_send, pair_recv,
     near_send, near_recv, far_send, far_recv, att_send, att_recv,
 ):
@@ -66,17 +67,27 @@
                 (clip, x.at[1, h]),
                 (w_time, wt),
                 (w_out, wo.at[0]),
-                (w_key, wk),
-                (w_value, wv),
-                (w_query, wq),
                 (gain, gains),
+            ]
+            + [
+                (weights.at[pl.ds(k * HEAD_SIZE, HEAD_SIZE)], dest.at[pl.ds((first + k) * LANES, HEAD_SIZE)])
+                for weights, dest, first in ((w_key, wkv, 0), (w_value, wkv, local_heads), (w_query, wq, 0))
+                for k in range(local_heads)
             ]
         )
     ]
+    rest = LANES - HEAD_SIZE
+    for dest in (wq, wkv):
+        for k in range(dest.shape[0] // LANES):
+            dest[pl.ds(k * LANES + HEAD_SIZE, rest), :] = jnp.zeros((rest, dest.shape[1]), BF16)
     for load in loads:
         load.start()
 
     tok[...] = jnp.zeros_like(tok)
+    values[:, :, LANES:] = jnp.ones((local_heads, tok.shape[1], LANES), BF16)
+    for k in range(2):
+        for i in range(local_heads):
+            wo_half[k, pl.ds(i * LANES + HEAD_SIZE, rest), :] = jnp.zeros((rest, half), BF16)
 
     @pl.when(f == 0)
     def _():
@@ -120,23 +131,20 @@
         remote(clip, x.at[1, h], pair_send.at[0], pair_recv.at[0], partner),
         remote(w_out, wo.at[1], pair_send.at[1], pair_recv.at[1], partner),
     ]
-    for copy in pair:
-        copy.start()
+    pair[0].start()
 
     def weight(o, which):
         return wt[o, pl.ds(pl.multiple_of(which * half, half), half), :]
+
+    def sides(which, rows):
+        both = jnp.concatenate([x[0, which, rows], x[2, which, rows]], axis=1)
+        return dot(both, jnp.concatenate([weight(0, which), weight(2, which)], axis=0))
 
     loads[1].wait()
     loads[2].wait()
     pair[0].wait_recv()
-    first = jnp.concatenate([x[1, 0].astype(F32), x[1, 1].astype(F32)], axis=1)
-    base[...] = first + dot(x[1, 0], wt[1, :half, :]) + dot(x[1, 1], wt[1, half:, :])
-
-    loads[3].wait()
-    pair[1].wait_recv()
-    for k in range(2):
-        whole = wo[k].astype(F32)
-        wo_half[k] = jnp.where(h == 0, whole[:, :half], whole[:, half:]).astype(BF16)
+    centre_full = jnp.concatenate([x[1, 0], x[1, 1]], axis=1)
+    base[...] = centre_full.astype(F32) + dot(centre_full, wt[1])
 
     loads[0].wait()
     for copy in near:
@@ -145,6 +153,16 @@
     far = [remote(line, line, far_send.at[a, b], far_recv.at[a, b], plane_to(a, b)) for a, b in plane]
     for copy in far:
         copy.start()
+    pair[1].start()
+
+    def prepare():
+        loads[3].wait()
+        pair[1].wait_recv()
+        for k in range(2):
+            whole = wo[k].astype(F32)
+            part = jnp.where(h == 0, whole[:, :half], whole[:, half:]).astype(BF16)
+            for i in range(local_heads):
+                wo_half[k, pl.ds(i * LANES, HEAD_SIZE), :] = part[i * HEAD_SIZE : (i + 1) * HEAD_SIZE, :]
 
     def arrive(c):
         for side in range(2):
@@ -153,7 +171,7 @@
                 halo(side, c).wait_recv()
                 relay(side, c).start()
         rows = rows_of(c)
-        base[rows] = base[rows] + dot(x[0, h, rows], weight(0, h)) + dot(x[2, h, rows], weight(2, h))
+        base[rows] = base[rows] + sides(h, rows)
 
     def make_keys():
         for copy in far:
@@ -168,19 +186,17 @@
                     return carry
 
                 lax.fori_loop(0, nr * nf, place, 0)
-        loads[4].wait()
-        loads[5].wait()
+        for load in loads[5:]:
+            load.wait()
         block = min(256, tok.shape[1])
 
         def project(i, carry):
             at = pl.ds(pl.multiple_of(i * block, block), block)
-            head = lax.broadcasted_iota(jnp.int32, (block, half), 1)
             both = jnp.concatenate([tok[k, at, :] for k in range(nh)], axis=1)
-            for weights, dest in ((wk, keys), (wv, values)):
-                full = dot_t(both, weights[...])
-                for k in range(local_heads):
-                    inside = (head >= k * HEAD_SIZE) & (head < (k + 1) * HEAD_SIZE)
-                    dest[k, at, :] = jnp.where(inside, full, 0.0).astype(BF16)
+            full = dot_t(both, wkv[...]).astype(BF16)
+            for k in range(local_heads):
+                keys[k, at, :] = full[:, k * LANES : (k + 1) * LANES]
+                values[k, at, :LANES] = full[:, (local_heads + k) * LANES : (local_heads + k + 1) * LANES]
             return carry
 
         trips = tok.shape[1] // block
@@ -188,12 +204,12 @@
             project(0, 0)
         else:
             lax.fori_loop(0, trips, project, 0)
-        loads[6].wait()
 
     scale = 1.0 / (HEAD_SIZE ** 0.5)
 
-    def attended(c):
-        return remote(att.at[0, rows_of(c)], att.at[1, rows_of(c)], att_send.at[c], att_recv.at[c], partner)
+    def attended(c, k):
+        rows = rows_of(c)
+        return remote(att.at[0, k, rows], att.at[1, k, rows], att_send.at[c, k], att_recv.at[c, k], partner)
 
     def process(c):
         rows = rows_of(c)
@@ -201,7 +217,7 @@
             @pl.when(gets[side])
             def _():
                 relay(side, c).wait_recv()
-        summed = base[rows] + dot(x[0, other, rows], weight(0, other)) + dot(x[2, other, rows], weight(2, other))
+        summed = base[rows] + sides(other, rows)
         feats = summed.astype(BF16).astype(F32)
         base[rows] = feats
         centre = jnp.mean(feats, axis=-1, keepdims=True)
@@ -213,36 +229,34 @@
         column = lax.broadcasted_iota(jnp.int32, (step, total_tokens), 1)
         valid = lax.rem(column, pad) < count
 
-        def attend(k, result):
-            scores = jnp.where(valid, dot_t(query, keys[k]), -3e38)
-            expo = jnp.exp(scores - jnp.max(scores, axis=1, keepdims=True))
-            total = jnp.sum(expo, axis=1, keepdims=True)
-            return result + dot(expo.astype(BF16), values[k]) * (1.0 / total)
-
-        result = jnp.zeros((step, half), F32)
-        if total_tokens <= 1024:
-            for k in range(local_heads):
-                result = attend(k, result)
-        else:
-            result = lax.fori_loop(0, local_heads, attend, result)
-        att[0, rows] = result.astype(BF16)
-        attended(c).start()
+        for k in range(local_heads):
+            scores = jnp.where(valid, dot_t(query[:, k * LANES : (k + 1) * LANES], keys[k]), -3e38)
+            probs = jnp.exp(scores - jnp.max(scores, axis=1, keepdims=True)).astype(BF16)
+            mixed = dot(probs, values[k])
+            att[0, k, rows] = (mixed[:, :LANES] / mixed[:, LANES:]).astype(BF16)
+            attended(c, k).start()
 
     def finish(c):
         rows = rows_of(c)
         feats = base[rows]
         own = jnp.where(h == 0, feats[:, :half], feats[:, half:])
-        mixed = own + dot(att[0, rows], wo_half[0])
-        attended(c).wait_recv()
-        out[rows] = (mixed + dot(att[1, rows], wo_half[1])).astype(BF16)
-
-    loads[7].wait()
+
+        def joined(which):
+            return jnp.concatenate([att[which, k, rows] for k in range(local_heads)], axis=1)
+
+        mixed = own + dot(joined(0), wo_half[0])
+        for k in range(local_heads):
+            attended(c, k).wait_recv()
+        out[rows] = (mixed + dot(joined(1), wo_half[1])).astype(BF16)
+
+    loads[4].wait()
     gain_row = gains[...].reshape(1, -1)
 
+    make_keys()
     arrive(0)
     for c in range(1, min(2, chunks)):
         arrive(c)
-    make_keys()
+    prepare()
     for c in range(chunks):
         process(c)
         if c + 2 < chunks:
@@ -254,7 +268,8 @@
     for copy in near + pair + far:
         copy.wait_send()
     for c in range(chunks):
-        attended(c).wait_send()
+        for k in range(local_heads):
+            attended(c, k).wait_send()
         for side in range(2):
             @pl.when(sends[side])
             def _():
@@ -271,7 +286,7 @@
     half, width = w_out.shape
     positions = shape[0] * shape[1] * shape[2]
     assert shape[0] == 1 and nh == 2
-    chunks = next(n for n in (3, 2, 1) if positions % (16 * n) == 0)
+    chunks = next(n for n in (1,) if positions % (16 * n) == 0)
     count = reference_tokens.shape[0]
     pad = -(-count // 16) * 16
     total = pad * nf * nr
@@ -285,19 +300,18 @@
         scratch_shapes=[
             pltpu.VMEM((3, 2, positions, half), BF16),
             pltpu.VMEM(w_time.shape, BF16),
-            pltpu.VMEM((half, width), BF16),
-            pltpu.VMEM((half, width), BF16),
-            pltpu.VMEM((half, width), BF16),
+            pltpu.VMEM((heads * LANES, width), BF16),
+            pltpu.VMEM((2 * heads * LANES, width), BF16),
             pltpu.VMEM((2, half, width), BF16),
-            pltpu.VMEM((2, half, half), BF16),
+            pltpu.VMEM((2, heads * LANES, half), BF16),
             pltpu.VMEM((width,), F32),
             pltpu.VMEM((nh, nr * nf, count, half), BF16),
             pltpu.VMEM((nh, total, half), BF16),
-            pltpu.VMEM((heads, total, half), BF16),
-            pltpu.VMEM((heads, total, half), BF16),
+            pltpu.VMEM((heads, total, LANES), BF16),
+            pltpu.VMEM((heads, total, 2 * LANES), BF16),
             pltpu.VMEM((positions, width), F32),
-            pltpu.VMEM((2, positions, half), BF16),
-            dma((8,)),
+            pltpu.VMEM((2, heads, positions, LANES), BF16),
+            dma((5 + 3 * heads,)),
             dma((2, chunks)),
             dma((2, chunks)),
             dma((2, chunks)),
@@ -308,8 +322,8 @@
             dma((nf,)),
             dma((nr, nh)),
             dma((nr, nh)),
-            dma((chunks,)),
-            dma((chunks,)),
+            dma((chunks, heads)),
+            dma((chunks, heads)),
         ],
         compiler_params=pltpu.CompilerParams(collective_id=0, has_side_effects=True),
     )(

time: 24.7 us -> 21 us (0.85)
  Pallas kernels: 22.9 us -> 19.1 us
    pallas_call x1, Pallas kernels: 22.9 us -> 19.1 us  [body(): pl.pallas_call(functools.partial(kernel, (nf, nr, nh, chunks, pad)), out_...]
where the time goes in v3:
time: 21 us; the launch traced here: 20.8 us
  Pallas kernels  19.1 us (91%)
  local copies, waits for them, and re-layouts  1.64 us (8%)
    pallas_call x1, Pallas kernels, body(): pl.pallas_call(functools.partial(kernel, (nf, nr, nh, chunks, pad)), out_...  19.1 us
    unnamed x1, local copies, waits for them, and re-layouts  1.64 us

profile of v3, /device:TPU:0, one launch (start us, length us, event | category | flops | bytes accessed | tf_op | source)
XLA Modules:
  0.0 20.8 jit_solution(14913047012685056592)
XLA Ops:
  0.0 19.1 %shard_map.82 = bf16[288,320]{1,0:T(8,128)(2,1)} custom-call(bf16[288,320]{1,0:T(8,128)(2,1)} %bitcast.9, f32[640]{0:T(1024)} %gain.1, bf16[3,640,640]{2,1,0:T(8,128)(2,1)} %w_time.1, bf16[320,640]{1,0:T(8,128)(2,1)} %bitcast.6, bf16[320,640]{1,0:T(8,128)(2,1)} %bitcast.7, bf16[320,640]{1,0:T(8,128)(2,1)} %bitcast.8, bf16[320,640]{1,0:T(8,128)(2,1)} %w_out.1, ...), custom_call_target="tpu_custom_call" | custom-call | tf_op jit(solution)/shard_map/pallas_call | solution.py:295
  19.1 1.6 %copy.10 = bf16[1,6,48,320]{3,2,1,0:T(8,128)(2,1)} copy(bf16[1,6,48,320]{3,2,1,0:T(8,128)(2,1)} %bitcast.5) | data formatting | bytes 368640

commit v4 on v3

--- a/solution.py
+++ b/solution.py
@@ -26,7 +26,7 @@
     sizes,
     clip, gain, w_time, w_query, w_key, w_value, w_out, tokens,
     out,
-    x, wt, wq, wkv, wo, wo_half, gains, slots, tok, keys, values, base, att,
+    x, wt, wq, wkv, wo, gains, slots, tok, keys, values, base, att,
     local_sem, halo_send, halo_recv, relay_send, relay_recv, pair_send, pair_recv,
     near_send, near_recv, far_send, far_recv, att_send, att_recv,
 ):
@@ -66,18 +66,17 @@
                 (tokens, slots.at[h, mine]),
                 (clip, x.at[1, h]),
                 (w_time, wt),
-                (w_out, wo.at[0]),
                 (gain, gains),
             ]
             + [
                 (weights.at[pl.ds(k * HEAD_SIZE, HEAD_SIZE)], dest.at[pl.ds((first + k) * LANES, HEAD_SIZE)])
-                for weights, dest, first in ((w_key, wkv, 0), (w_value, wkv, local_heads), (w_query, wq, 0))
+                for weights, dest, first in ((w_key, wkv, 0), (w_value, wkv, local_heads), (w_query, wq, 0), (w_out, wo, 0))
                 for k in range(local_heads)
             ]
         )
     ]
     rest = LANES - HEAD_SIZE
-    for dest in (wq, wkv):
+    for dest in (wq, wkv, wo):
         for k in range(dest.shape[0] // LANES):
             dest[pl.ds(k * LANES + HEAD_SIZE, rest), :] = jnp.zeros((rest, dest.shape[1]), BF16)
     for load in loads:
@@ -85,9 +84,6 @@
 
     tok[...] = jnp.zeros_like(tok)
     values[:, :, LANES:] = jnp.ones((local_heads, tok.shape[1], LANES), BF16)
-    for k in range(2):
-        for i in range(local_heads):
-            wo_half[k, pl.ds(i * LANES + HEAD_SIZE, rest), :] = jnp.zeros((rest, half), BF16)
 
     @pl.when(f == 0)
     def _():
@@ -127,10 +123,7 @@
             def _():
                 halo(side, c).start()
 
-    pair = [
-        remote(clip, x.at[1, h], pair_send.at[0], pair_recv.at[0], partner),
-        remote(w_out, wo.at[1], pair_send.at[1], pair_recv.at[1], partner),
-    ]
+    pair = [remote(clip, x.at[1, h], pair_send.at[0], pair_recv.at[0], partner)]
     pair[0].start()
 
     def weight(o, which):
@@ -153,16 +146,6 @@
     far = [remote(line, line, far_send.at[a, b], far_recv.at[a, b], plane_to(a, b)) for a, b in plane]
     for copy in far:
         copy.start()
-    pair[1].start()
-
-    def prepare():
-        loads[3].wait()
-        pair[1].wait_recv()
-        for k in range(2):
-            whole = wo[k].astype(F32)
-            part = jnp.where(h == 0, whole[:, :half], whole[:, half:]).astype(BF16)
-            for i in range(local_heads):
-                wo_half[k, pl.ds(i * LANES, HEAD_SIZE), :] = part[i * HEAD_SIZE : (i + 1) * HEAD_SIZE, :]
 
     def arrive(c):
         for side in range(2):
@@ -186,7 +169,7 @@
                     return carry
 
                 lax.fori_loop(0, nr * nf, place, 0)
-        for load in loads[5:]:
+        for load in loads[4:]:
             load.wait()
         block = min(256, tok.shape[1])
 
@@ -207,9 +190,9 @@
 
     scale = 1.0 / (HEAD_SIZE ** 0.5)
 
-    def attended(c, k):
+    def share(c):
         rows = rows_of(c)
-        return remote(att.at[0, k, rows], att.at[1, k, rows], att_send.at[c, k], att_recv.at[c, k], partner)
+        return remote(att.at[0, rows], att.at[1, rows], att_send.at[c], att_recv.at[c], partner)
 
     def process(c):
         rows = rows_of(c)
@@ -229,34 +212,31 @@
         column = lax.broadcasted_iota(jnp.int32, (step, total_tokens), 1)
         valid = lax.rem(column, pad) < count
 
+        attended = []
         for k in range(local_heads):
             scores = jnp.where(valid, dot_t(query[:, k * LANES : (k + 1) * LANES], keys[k]), -3e38)
             probs = jnp.exp(scores - jnp.max(scores, axis=1, keepdims=True)).astype(BF16)
             mixed = dot(probs, values[k])
-            att[0, k, rows] = (mixed[:, :LANES] / mixed[:, LANES:]).astype(BF16)
-            attended(c, k).start()
+            attended.append((mixed[:, :LANES] / mixed[:, LANES:]).astype(BF16))
+        mixed = dot(jnp.concatenate(attended, axis=1), wo[...])
+        low, high = mixed[:, :half], mixed[:, half:]
+        att[0, rows] = jnp.where(h == 0, high, low).astype(BF16)
+        share(c).start()
+        total = base[rows] + mixed
+        base[rows, :half] = jnp.where(h == 0, total[:, :half], total[:, half:])
 
     def finish(c):
         rows = rows_of(c)
-        feats = base[rows]
-        own = jnp.where(h == 0, feats[:, :half], feats[:, half:])
-
-        def joined(which):
-            return jnp.concatenate([att[which, k, rows] for k in range(local_heads)], axis=1)
-
-        mixed = own + dot(joined(0), wo_half[0])
-        for k in range(local_heads):
-            attended(c, k).wait_recv()
-        out[rows] = (mixed + dot(joined(1), wo_half[1])).astype(BF16)
-
-    loads[4].wait()
+        share(c).wait_recv()
+        out[rows] = (base[rows, :half] + att[1, rows].astype(F32)).astype(BF16)
+
+    loads[3].wait()
     gain_row = gains[...].reshape(1, -1)
 
     make_keys()
     arrive(0)
     for c in range(1, min(2, chunks)):
         arrive(c)
-    prepare()
     for c in range(chunks):
         process(c)
         if c + 2 < chunks:
@@ -268,8 +248,7 @@
     for copy in near + pair + far:
         copy.wait_send()
     for c in range(chunks):
-        for k in range(local_heads):
-            attended(c, k).wait_send()
+        share(c).wait_send()
         for side in range(2):
             @pl.when(sends[side])
             def _():
@@ -302,28 +281,27 @@
             pltpu.VMEM(w_time.shape, BF16),
             pltpu.VMEM((heads * LANES, width), BF16),
             pltpu.VMEM((2 * heads * LANES, width), BF16),
-            pltpu.VMEM((2, half, width), BF16),
-            pltpu.VMEM((2, heads * LANES, half), BF16),
+            pltpu.VMEM((heads * LANES, width), BF16),
             pltpu.VMEM((width,), F32),
             pltpu.VMEM((nh, nr * nf, count, half), BF16),
             pltpu.VMEM((nh, total, half), BF16),
             pltpu.VMEM((heads, total, LANES), BF16),
             pltpu.VMEM((heads, total, 2 * LANES), BF16),
             pltpu.VMEM((positions, width), F32),
-            pltpu.VMEM((2, heads, positions, LANES), BF16),
-            dma((5 + 3 * heads,)),
+            pltpu.VMEM((2, positions, half), BF16),
+            dma((4 + 4 * heads,)),
             dma((2, chunks)),
             dma((2, chunks)),
             dma((2, chunks)),
             dma((2, chunks)),
-            dma((2,)),
-            dma((2,)),
+            dma((1,)),
+            dma((1,)),
             dma((nf,)),
             dma((nf,)),
             dma((nr, nh)),
             dma((nr, nh)),
-            dma((chunks, heads)),
-            dma((chunks, heads)),
+            dma((chunks,)),
+            dma((chunks,)),
         ],
         compiler_params=pltpu.CompilerParams(collective_id=0, has_side_effects=True),
     )(

time: 21 us -> 20.4 us (0.971)
  Pallas kernels: 19.1 us -> 18.6 us
    pallas_call x1, Pallas kernels: 19.1 us -> 18.6 us  [body(): pl.pallas_call(functools.partial(kernel, (nf, nr, nh, chunks, pad)), out_...]
where the time goes in v4:
time: 20.4 us; the launch traced here: 20.2 us
  Pallas kernels  18.6 us (91%)
  local copies, waits for them, and re-layouts  1.64 us (8%)
    pallas_call x1, Pallas kernels, body(): pl.pallas_call(functools.partial(kernel, (nf, nr, nh, chunks, pad)), out_...  18.6 us
    unnamed x1, local copies, waits for them, and re-layouts  1.64 us

profile of v4, /device:TPU:0, one launch (start us, length us, event | category | flops | bytes accessed | tf_op | source)
XLA Modules:
  0.0 20.2 jit_solution(13534532067809098151)
XLA Ops:
  0.0 18.6 %shard_map.82 = bf16[288,320]{1,0:T(8,128)(2,1)} custom-call(bf16[288,320]{1,0:T(8,128)(2,1)} %bitcast.9, f32[640]{0:T(1024)} %gain.1, bf16[3,640,640]{2,1,0:T(8,128)(2,1)} %w_time.1, bf16[320,640]{1,0:T(8,128)(2,1)} %bitcast.6, bf16[320,640]{1,0:T(8,128)(2,1)} %bitcast.7, bf16[320,640]{1,0:T(8,128)(2,1)} %bitcast.8, bf16[320,640]{1,0:T(8,128)(2,1)} %w_out.1, ...), custom_call_target="tpu_custom_call" | custom-call | tf_op jit(solution)/shard_map/pallas_call | solution.py:274
  18.6 1.6 %copy.10 = bf16[1,6,48,320]{3,2,1,0:T(8,128)(2,1)} copy(bf16[1,6,48,320]{3,2,1,0:T(8,128)(2,1)} %bitcast.5) | data formatting | bytes 368640

commit v5 on v4

--- a/solution.py
+++ b/solution.py
@@ -26,7 +26,7 @@
     sizes,
     clip, gain, w_time, w_query, w_key, w_value, w_out, tokens,
     out,
-    x, wt, wq, wkv, wo, gains, slots, tok, keys, values, base, att,
+    x, wt, wq, wkv, wqt, wkvt, wo, gains, slots, tok, keys, values, base, att,
     local_sem, halo_send, halo_recv, relay_send, relay_recv, pair_send, pair_recv,
     near_send, near_recv, far_send, far_recv, att_send, att_recv,
 ):
@@ -79,7 +79,7 @@
     for dest in (wq, wkv, wo):
         for k in range(dest.shape[0] // LANES):
             dest[pl.ds(k * LANES + HEAD_SIZE, rest), :] = jnp.zeros((rest, dest.shape[1]), BF16)
-    for load in loads:
+    for load in loads[:2] + loads[3:] + loads[2:3]:
         load.start()
 
     tok[...] = jnp.zeros_like(tok)
@@ -133,12 +133,10 @@
         both = jnp.concatenate([x[0, which, rows], x[2, which, rows]], axis=1)
         return dot(both, jnp.concatenate([weight(0, which), weight(2, which)], axis=0))
 
-    loads[1].wait()
-    loads[2].wait()
-    pair[0].wait_recv()
-    centre_full = jnp.concatenate([x[1, 0], x[1, 1]], axis=1)
-    base[...] = centre_full.astype(F32) + dot(centre_full, wt[1])
-
+    for load in loads[4:]:
+        load.wait()
+    wkvt[...] = wkv[...].T
+    wqt[...] = wq[...].T
     loads[0].wait()
     for copy in near:
         copy.wait_recv()
@@ -146,6 +144,12 @@
     far = [remote(line, line, far_send.at[a, b], far_recv.at[a, b], plane_to(a, b)) for a, b in plane]
     for copy in far:
         copy.start()
+
+    loads[1].wait()
+    loads[2].wait()
+    pair[0].wait_recv()
+    centre_full = jnp.concatenate([x[1, 0], x[1, 1]], axis=1)
+    base[...] = centre_full.astype(F32) + dot(centre_full, wt[1])
 
     def arrive(c):
         for side in range(2):
@@ -169,14 +173,12 @@
                     return carry
 
                 lax.fori_loop(0, nr * nf, place, 0)
-        for load in loads[4:]:
-            load.wait()
         block = min(256, tok.shape[1])
 
         def project(i, carry):
             at = pl.ds(pl.multiple_of(i * block, block), block)
             both = jnp.concatenate([tok[k, at, :] for k in range(nh)], axis=1)
-            full = dot_t(both, wkv[...]).astype(BF16)
+            full = dot(both, wkvt[...]).astype(BF16)
             for k in range(local_heads):
                 keys[k, at, :] = full[:, k * LANES : (k + 1) * LANES]
                 values[k, at, :LANES] = full[:, (local_heads + k) * LANES : (local_heads + k + 1) * LANES]
@@ -207,7 +209,7 @@
         moved = feats - centre
         spread = jnp.mean(moved * moved, axis=-1, keepdims=True)
         normed = (moved * lax.rsqrt(spread + 1e-05) * gain_row).astype(BF16)
-        query = (dot_t(normed, wq[...]) * scale).astype(BF16)
+        query = (dot(normed, wqt[...]) * scale).astype(BF16)
         total_tokens = tok.shape[1]
         column = lax.broadcasted_iota(jnp.int32, (step, total_tokens), 1)
         valid = lax.rem(column, pad) < count
@@ -281,6 +283,8 @@
             pltpu.VMEM(w_time.shape, BF16),
             pltpu.VMEM((heads * LANES, width), BF16),
             pltpu.VMEM((2 * heads * LANES, width), BF16),
+            pltpu.VMEM((width, heads * LANES), BF16),
+            pltpu.VMEM((width, 2 * heads * LANES), BF16),
             pltpu.VMEM((heads * LANES, width), BF16),
             pltpu.VMEM((width,), F32),
             pltpu.VMEM((nh, nr * nf, count, half), BF16),

time: 20.4 us -> 20.2 us (level)
  no operation moved by 1% of the time
where the time goes in v5:
time: 20.2 us; the launch traced here: 20.1 us
  Pallas kernels  18.4 us (91%)
  local copies, waits for them, and re-layouts  1.64 us (8%)
    pallas_call x1, Pallas kernels, body(): pl.pallas_call(functools.partial(kernel, (nf, nr, nh, chunks, pad)), out_...  18.4 us
    unnamed x1, local copies, waits for them, and re-layouts  1.64 us

profile of v5, /device:TPU:0, one launch (start us, length us, event | category | flops | bytes accessed | tf_op | source)
XLA Modules:
  0.0 20.1 jit_solution(10622926814447316262)
XLA Ops:
  0.0 18.4 %shard_map.82 = bf16[288,320]{1,0:T(8,128)(2,1)} custom-call(bf16[288,320]{1,0:T(8,128)(2,1)} %bitcast.9, f32[640]{0:T(1024)} %gain.1, bf16[3,640,640]{2,1,0:T(8,128)(2,1)} %w_time.1, bf16[320,640]{1,0:T(8,128)(2,1)} %bitcast.6, bf16[320,640]{1,0:T(8,128)(2,1)} %bitcast.7, bf16[320,640]{1,0:T(8,128)(2,1)} %bitcast.8, bf16[320,640]{1,0:T(8,128)(2,1)} %w_out.1, ...), custom_call_target="tpu_custom_call" | custom-call | tf_op jit(solution)/shard_map/pallas_call | solution.py:276
  18.4 1.6 %copy.10 = bf16[1,6,48,320]{3,2,1,0:T(8,128)(2,1)} copy(bf16[1,6,48,320]{3,2,1,0:T(8,128)(2,1)} %bitcast.5) | data formatting | bytes 368640
